TPU v7x, 32 devices: a whole 2x2x4 slice. The times are simulated.
32 devices in a mesh: expert: 8 (over z, y), replica: 4 (over x, core).
Axes of the slice: x: 2, y: 2, z: 4, core: 2. Of those that a mesh axis runs over, the one named last changes fastest.
Arguments:
- tokens: bfloat16 [4096, 2048], P(('expert', 'replica')), may hold values from -6 to 6
- out_grad: bfloat16 [4096, 2048], P(('expert', 'replica')), may hold values from -6 to 6
- expert_ids: int32 [4096, 2], P(('expert', 'replica')), may hold values from 0 to 3, as said below
- route_weights: bfloat16 [4096, 2], P(('expert', 'replica')), may hold values from 0.25 to 1
- capacity: int32 [4], replicated, may hold values from 2 to 2
- w_gate: bfloat16 [8, 2048, 384], P('expert', 'replica'), may hold values from -0.125 to 0.125
- w_up: bfloat16 [8, 2048, 384], P('expert', 'replica'), may hold values from -0.125 to 0.125
- w_down: bfloat16 [8, 384, 2048], P('expert', None, 'replica'), may hold values from -0.21875 to 0.21875
Outputs:
- x_grad: bfloat16 [4096, 2048], P(('expert', 'replica'))
- gate_grad: bfloat16 [8, 2048, 384], P('expert', 'replica')
- up_grad: bfloat16 [8, 2048, 384], P('expert', 'replica')
- down_grad: bfloat16 [8, 384, 2048], P('expert')
Inputs may be any that keep to these rules, and one draw needn't show every extreme that they name: `expert_ids`: each row names 2 different experts.
All inputs are finite; a program needn't handle non-finite values.
Results may differ from a plain program's by a relative error of at most 0.009.
Values may be sent and summed in bfloat16 or wider, within the bound.
A program may use at most 64 MiB of HBM per device.

v0:
```python
import jax
import jax.numpy as jnp
from jax import lax
from jax.sharding import PartitionSpec as P

CAP = 2


def shards(tokens, out_grad, expert_ids, route_weights, capacity, w_gate, w_up, w_down):
    experts = capacity.shape[0]
    owners = lax.axis_size("expert")
    width = tokens.shape[1]
    slot_count = experts * CAP
    expert_range = jnp.arange(experts, dtype=jnp.int32)
    chosen = (expert_ids[:, :, None] == expert_range[None, None, :]).astype(jnp.int32)
    ranks = jnp.cumsum(jnp.sum(chosen, axis=1), axis=0)
    place = jnp.sum(chosen * ranks[:, None, :], axis=2) - 1
    limit = jnp.sum(chosen * capacity[None, None, :], axis=2)
    slot_ids = jnp.where(place < limit, expert_ids * CAP + place, -1)
    table = slot_ids[None, :, :] == jnp.arange(slot_count, dtype=jnp.int32)[:, None, None]
    picker = jnp.any(table, axis=2).astype(jnp.bfloat16)
    slot_weight = jnp.sum(
        jnp.where(table, route_weights.astype(jnp.float32)[None, :, :], 0.0), axis=(1, 2)
    ).astype(jnp.bfloat16)
    packed = jnp.dot(
        picker, jnp.concatenate([tokens, out_grad], axis=1), preferred_element_type=jnp.float32
    ).astype(jnp.bfloat16)
    packed = packed.reshape(experts, CAP, 2 * width)
    slot_weight = slot_weight.reshape(experts, CAP)
    send_rows = jnp.broadcast_to(packed[:, None], (experts, 2, CAP, 2 * width)).reshape(
        owners, CAP, 2 * width
    )
    send_weight = jnp.broadcast_to(slot_weight[:, None], (experts, 2, CAP)).reshape(owners, CAP)
    got_rows, got_weight = (
        lax.all_to_all(send_rows, "expert", split_axis=0, concat_axis=0, tiled=True),
        lax.all_to_all(send_weight, "expert", split_axis=0, concat_axis=0, tiled=True),
    )
    gate_all, up_all, down_all = (
        lax.all_gather(w_gate, "replica", axis=1, tiled=True),
        lax.all_gather(w_up, "replica", axis=1, tiled=True),
        lax.all_gather(w_down, "replica", axis=2, tiled=True),
    )
    gate_mat = gate_all[0]
    up_mat = up_all[0]
    down_mat = down_all[0]
    row_total = owners * CAP
    flat_rows = got_rows.reshape(row_total, 2 * width)
    inputs = flat_rows[:, :width]
    cotangent = flat_rows[:, width:]
    weights = got_weight.reshape(row_total).astype(jnp.float32)
    gate = jnp.dot(inputs, gate_mat, preferred_element_type=jnp.float32)
    up = jnp.dot(inputs, up_mat, preferred_element_type=jnp.float32)
    sig = jax.nn.sigmoid(gate)
    act = gate * sig
    hidden = (act * up).astype(jnp.bfloat16)
    scaled = (weights[:, None] * cotangent.astype(jnp.float32)).astype(jnp.bfloat16)
    back = lax.dot_general(
        scaled, down_mat, (((1,), (1,)), ((), ())), preferred_element_type=jnp.float32
    )
    gate_back = (back * up * sig * (1.0 + gate * (1.0 - sig))).astype(jnp.bfloat16)
    up_back = (back * act).astype(jnp.bfloat16)
    both_back = jnp.concatenate([gate_back, up_back], axis=1)
    both_mat = jnp.concatenate([gate_mat, up_mat], axis=1)
    partial_value = lax.dot_general(
        both_back, both_mat, (((1,), (1,)), ((), ())), preferred_element_type=jnp.float32
    ).astype(jnp.bfloat16)
    returned = lax.all_to_all(
        partial_value.reshape(owners, CAP, width), "expert", split_axis=0, concat_axis=0, tiled=True
    )
    returned = returned.reshape(experts, 2, CAP, width)
    total = lax.dot_general(
        picker,
        returned[:, 0].reshape(slot_count, width),
        (((0,), (0,)), ((), ())),
        preferred_element_type=jnp.float32,
    )
    total = total + lax.dot_general(
        picker,
        returned[:, 1].reshape(slot_count, width),
        (((0,), (0,)), ((), ())),
        preferred_element_type=jnp.float32,
    )
    x_grad = total.astype(jnp.bfloat16)
    wide_grad = lax.psum_scatter(
        lax.dot_general(
            inputs, both_back, (((0,), (0,)), ((), ())), preferred_element_type=jnp.float32
        )
        .astype(jnp.bfloat16)
        .astype(jnp.bfloat16),
        "replica",
        scatter_dimension=0,
        tiled=True,
    ).astype(jnp.float32)
    half_units = gate_mat.shape[1]
    gate_grad = wide_grad[:, :half_units].astype(jnp.bfloat16)[None]
    up_grad = wide_grad[:, half_units:].astype(jnp.bfloat16)[None]
    down_local = lax.dot_general(
        hidden, scaled, (((0,), (0,)), ((), ())), preferred_element_type=jnp.float32
    )
    down_grad = lax.psum(down_local.astype(jnp.bfloat16), "replica")[None]
    return (x_grad, gate_grad, up_grad, down_grad)


def solution(mesh):
    return jax.shard_map(
        shards,
        mesh=mesh,
        in_specs=(
            P(("expert", "replica"), None),
            P(("expert", "replica"), None),
            P(("expert", "replica"), None),
            P(("expert", "replica"), None),
            P(),
            P("expert", "replica", None),
            P("expert", "replica", None),
            P("expert", None, "replica"),
        ),
        out_specs=(
            P(("expert", "replica"), None),
            P("expert", "replica", None),
            P("expert", "replica", None),
            P("expert", None, None),
        ),
        check_vma=False,
    )
```

profile of v0, /device:TPU:0, one launch (start us, length us, event | category | flops | bytes accessed | tf_op | source)
XLA Modules:
  0.0 171.9 jit_solution(11029008983379027724)
XLA Ops:
  7.2 0.7 all-gather.6.cloned.1.call-update
  7.9 0.7 all-gather.4.cloned.1.call-update
  8.7 0.7 all-gather.8.cloned.1.call-update
  9.4 0.7 convert_reduce_fusion.1
  10.4 0.7 convert_element_type.61
  11.1 0.8 select_reduce_fusion.2
  11.9 0.7 compare_select_fusion
  13.0 0.7 copy.30
  13.7 7.3 %all-to-all-start = ((bf16[8,1,2]{2,1,0:T(2,128)(2,1)}), bf16[8,1,2]{2,1,0:T(2,128)(2,1)S(1)}, u32[]{:S(2)}, u32[]{:S(2)}) async-start(bf16[8,1,2]{2,1,0:T(2,128)(2,1)} %copy.30), calls=%async_computation | async-start | bytes 8192 | tf_op jit(solution)/shard_map/all_to_all | solution.py:36
  21.0 1.4 convolution_convert_fusion
  22.6 4.9 %all-to-all-done = bf16[8,1,2]{2,1,0:T(2,128)(2,1)S(1)} async-done(((bf16[8,1,2]{2,1,0:T(2,128)(2,1)}), bf16[8,1,2]{2,1,0:T(2,128)(2,1)S(1)}, u32[]{:S(2)}, u32[]{:S(2)}) %all-to-all-start) | async-done | bytes 64 | tf_op jit(solution)/shard_map/all_to_all | solution.py:36
  27.5 0.7 broadcast_in_dim.47
  28.2 3.4 %all-to-all-start.1 = ((bf16[8,2,4096]{2,1,0:T(2,128)(2,1)}), bf16[8,2,4096]{2,1,0:T(2,128)(2,1)S(1)}, u32[]{:S(2)}, u32[]{:S(2)}) async-start(bf16[8,2,4096]{2,1,0:T(2,128)(2,1)} %bitcast), calls=%async_computation.1 | async-start | bytes 262144 | tf_op jit(solution)/shard_map/all_to_all | solution.py:35
  31.7 7.1 %all-to-all-done.1 = bf16[8,2,4096]{2,1,0:T(2,128)(2,1)S(1)} async-done(((bf16[8,2,4096]{2,1,0:T(2,128)(2,1)}), bf16[8,2,4096]{2,1,0:T(2,128)(2,1)S(1)}, u32[]{:S(2)}, u32[]{:S(2)}) %all-to-all-start.1) | async-done | bytes 131104 | tf_op jit(solution)/shard_map/all_to_all | solution.py:35
  38.9 1.8 %fusion.17 = f32[16,384]{1,0:T(8,128)S(1)} fusion(bf16[16,4096]{1,0:T(8,128)(2,1)S(1)} %reshape.48, bf16[1,2048,384]{2,1,0:T(8,128)(2,1)} %all-gather.6.cloned.1.call-done), kind=kOutput, calls=%fused_computation.22 | convolution fusion | flops 25165824 | bytes 1662976 | tf_op jit(solution)/shard_map/dot_general | solution.py:52
  40.7 12.4 %all-gather.4.cloned.1.call-done = bf16[1,384,2048]{2,1,0:T(8,128)(2,1)} async-done(((bf16[1,384,512]{2,1,0:T(8,128)(2,1)}), bf16[1,384,2048]{2,1,0:T(8,128)(2,1)}) %all-gather.4.cloned.1.call-update) | async-done | bytes 1572880 | tf_op jit(solution)/shard_map/all_gather | solution.py:41
  53.1 1.9 %fusion.9 = f32[16,384]{1,0:T(8,128)S(1)} fusion(bf16[1,384,2048]{2,1,0:T(8,128)(2,1)} %all-gather.4.cloned.1.call-done, bf16[16,4096]{1,0:T(8,128)(2,1)S(1)} %reshape.48, f32[16]{0:T(128)S(1)} %reshape.51), kind=kOutput, calls=%fused_computation.11 | convolution fusion | flops 25264128 | bytes 1663488 | tf_op jit(solution)/shard_map/dot_general | solution.py:57
  55.1 19.3 %all-gather.8.cloned.1.call-done = bf16[1,2048,384]{2,1,0:T(8,128)(2,1)} async-done(((bf16[1,512,384]{2,1,0:T(8,128)(2,1)}), bf16[1,2048,384]{2,1,0:T(8,128)(2,1)}) %all-gather.8.cloned.1.call-update) | async-done | bytes 1572880 | tf_op jit(solution)/shard_map/all_gather | solution.py:39
  74.4 1.7 %multiply_convert_fusion.3 = (bf16[16,384]{1,0:T(8,128)(2,1)S(1)}, bf16[16,384]{1,0:T(8,128)(2,1)S(1)}, f32[16,384]{1,0:T(8,128)S(1)}) fusion(f32[16,384]{1,0:T(8,128)S(1)} %fusion.9, f32[16,384]{1,0:T(8,128)S(1)} %fusion.17, bf16[1,2048,384]{2,1,0:T(8,128)(2,1)} %all-gather.8.cloned.1.call-done, bf16[16,4096]{1,0:T(8,128)(2,1)S(1)} %reshape.48), kind=kOutput, calls=%fused_computation.27 | convolution fusion | flops 25245696 | bytes 1736704 | tf_op jit(solution)/shard_map/dot_general | solution.py:51
  76.1 2.7 %convolution_convert_fusion.1 = bf16[2048,768]{1,0:T(8,128)(2,1)} fusion(bf16[16,4096]{1,0:T(8,128)(2,1)S(1)} %reshape.48, bf16[16,384]{1,0:T(8,128)(2,1)S(1)} %get-tuple-element.11, bf16[16,384]{1,0:T(8,128)(2,1)S(1)} %get-tuple-element.10), kind=kOutput, calls=%fused_computation.1 | convolution fusion | flops 51953664 | bytes 3235840 | tf_op jit(solution)/shard_map/dot_general | solution.py:85
  78.8 1.4 copy-done
  80.2 0.5 copy-done.1
  80.7 0.9 fusion.6
  81.6 0.7 reshape.49
  82.3 5.5 %all-to-all-start.2 = ((bf16[8,2,2048]{2,1,0:T(2,128)(2,1)}), bf16[8,2,2048]{2,1,0:T(2,128)(2,1)S(1)}, u32[]{:S(2)}, u32[]{:S(2)}) async-start(bf16[8,2,2048]{2,1,0:T(2,128)(2,1)} %reshape.49), calls=%async_computation.2 | async-start | bytes 131072 | tf_op jit(solution)/shard_map/all_to_all | solution.py:67
  87.9 1.8 %fusion.4 = bf16[1,384,2048]{2,1,0:T(8,128)(2,1)} fusion(bf16[16,4096]{1,0:T(8,128)(2,1)S(1)} %reshape.48, f32[16]{0:T(128)S(1)} %reshape.51, f32[16,384]{1,0:T(8,128)S(1)} %fusion.17, f32[16,384]{1,0:T(8,128)S(1)} %get-tuple-element.12), kind=kOutput, calls=%fused_computation.7 | convolution fusion | flops 26087424 | bytes 1688064 | tf_op jit(solution)/shard_map/dot_general | solution.py:97
  89.7 5.1 %all-to-all-done.2 = bf16[8,2,2048]{2,1,0:T(2,128)(2,1)S(1)} async-done(((bf16[8,2,2048]{2,1,0:T(2,128)(2,1)}), bf16[8,2,2048]{2,1,0:T(2,128)(2,1)S(1)}, u32[]{:S(2)}, u32[]{:S(2)}) %all-to-all-start.2) | async-done | bytes 65568 | tf_op jit(solution)/shard_map/all_to_all | solution.py:67
  95.2 1.1 fusion.5
  96.3 20.6 %reduce-scatter.2.cloned.1.call-done = bf16[512,768]{1,0:T(8,128)(2,1)} async-done(((bf16[2048,768]{1,0:T(8,128)(2,1)}), bf16[512,768]{1,0:T(8,128)(2,1)}) %reduce-scatter.2.cloned.1.call-update) | async-done | bytes 786448 | tf_op jit(solution)/shard_map/reduce_scatter | solution.py:84
  116.9 2.1 %slice_bitcast_fusion = (bf16[1,512,384]{2,1,0:T(8,128)(2,1)}, bf16[1,512,384]{2,1,0:T(8,128)(2,1)}) fusion(bf16[512,768]{1,0:T(8,128)(2,1)} %reduce-scatter.2.cloned.1.call-done), kind=kLoop, calls=%fused_computation.16 | loop fusion | bytes 1572864 | tf_op jit(solution)/shard_map/broadcast_in_dim | solution.py:96
  119.0 43.6 %all-reduce.2.cloned.1.call-done = bf16[1,384,2048]{2,1,0:T(8,128)(2,1)} async-done(((bf16[1,384,2048]{2,1,0:T(8,128)(2,1)}), bf16[1,384,2048]{2,1,0:T(8,128)(2,1)}) %all-reduce.2.cloned.1.call-update) | async-done | bytes 1572880 | tf_op jit(solution)/shard_map/psum | solution.py:100
  162.6 2.7 %copy.32 = bf16[1,384,2048]{2,1,0:T(8,128)(2,1)} copy(bf16[1,384,2048]{2,1,0:T(8,128)(2,1)} %all-reduce.2.cloned.1.call-done) | data formatting | bytes 3145728
  (27 shorter events, 1.7 us)
Async XLA Ops:
  7.2 31.8 %all-gather.6.cloned.1.call-start = ((), (), s32[]{:S(2)}) async-start(), calls=%async_computation.5 | async-start | bytes 1966080 | tf_op jit(solution)/shard_map/all_gather | solution.py:40
  7.9 45.2 %all-gather.4.cloned.1.call-start = ((), (), s32[]{:S(2)}) async-start(), calls=%async_computation.4 | async-start | bytes 1966080 | tf_op jit(solution)/shard_map/all_gather | solution.py:41
  8.6 65.7 %all-gather.8.cloned.1.call-start = ((), (), s32[]{:S(2)}) async-start(), calls=%async_computation.6 | async-start | bytes 1966080 | tf_op jit(solution)/shard_map/all_gather | solution.py:39
  13.7 13.7 %all-to-all-start = ((bf16[8,1,2]{2,1,0:T(2,128)(2,1)}), bf16[8,1,2]{2,1,0:T(2,128)(2,1)S(1)}, u32[]{:S(2)}, u32[]{:S(2)}) async-start(bf16[8,1,2]{2,1,0:T(2,128)(2,1)} %copy.30), calls=%async_computation | async-start | bytes 8192 | tf_op jit(solution)/shard_map/all_to_all | solution.py:36
  28.2 10.7 %all-to-all-start.1 = ((bf16[8,2,4096]{2,1,0:T(2,128)(2,1)}), bf16[8,2,4096]{2,1,0:T(2,128)(2,1)S(1)}, u32[]{:S(2)}, u32[]{:S(2)}) async-start(bf16[8,2,4096]{2,1,0:T(2,128)(2,1)} %bitcast), calls=%async_computation.1 | async-start | bytes 262144 | tf_op jit(solution)/shard_map/all_to_all | solution.py:35
  31.6 85.4 %reduce-scatter.2.cloned.1.call-start = ((), (), s32[]{:S(2)}) async-start(), calls=%async_computation.7 | async-start | bytes 3932160 | tf_op jit(solution)/shard_map/reduce_scatter | solution.py:84
  78.8 1.4 copy-start
  78.8 1.9 %copy-start.1 = (bf16[1,2048,384]{2,1,0:T(8,128)(2,1)S(1)}, bf16[1,2048,384]{2,1,0:T(8,128)(2,1)}, u32[]{:S(2)}) copy-start(bf16[1,2048,384]{2,1,0:T(8,128)(2,1)} %all-gather.8.cloned.1.call-done) | copy-start | bytes 4718596
  82.3 12.4 %all-to-all-start.2 = ((bf16[8,2,2048]{2,1,0:T(2,128)(2,1)}), bf16[8,2,2048]{2,1,0:T(2,128)(2,1)S(1)}, u32[]{:S(2)}, u32[]{:S(2)}) async-start(bf16[8,2,2048]{2,1,0:T(2,128)(2,1)} %reshape.49), calls=%async_computation.2 | async-start | bytes 131072 | tf_op jit(solution)/shard_map/all_to_all | solution.py:67
  87.8 74.8 %all-reduce.2.cloned.1.call-start = ((), (), s32[]{:S(2)}) async-start(), calls=%async_computation.8 | async-start | bytes 3145728 | tf_op jit(solution)/shard_map/psum | solution.py:100
Sparse Core Ops, SparseCore 0:
  9.5 22.3 all-gather.5
  33.5 19.6 all-gather.3
  54.7 19.6 all-gather.7
  79.0 37.9 reduce-scatter.1
  119.7 42.8 all-reduce.1
where the time goes:
time: 172 us
  waiting for transfers between devices  115 us (67%)
  starting transfers between devices  16.4 us (10%)
  between operations  13.9 us (8%)
  matrix products  13.7 us (8%)
  local copies, waits for them, and re-layouts  9.59 us (6%)
  other arithmetic  3.13 us (2%)
    psum x1, waiting for transfers between devices, shards(): down_grad = lax.psum(down_local.astype(jnp.bfloat16), 'replica')[None]  43.6 us
    reduce_scatter x1, waiting for transfers between devices, shards(): lax.psum_scatter(lax.dot_general(inputs, both_back, (((0,), (0,)), ((), (...  20.6 us
    all_gather x1, waiting for transfers between devices, shards(): lax.all_gather(w_gate, 'replica', axis=1, tiled=True)  19.3 us
    all_gather x1, waiting for transfers between devices, shards(): lax.all_gather(w_down, 'replica', axis=2, tiled=True)  12.4 us
    all_to_all x1, starting transfers between devices, shards(): lax.all_to_all(send_weight, 'expert', split_axis=0, concat_axis=0, tiled=...  7.31 us
    all_to_all x1, waiting for transfers between devices, shards(): lax.all_to_all(send_rows, 'expert', split_axis=0, concat_axis=0, tiled=True)  7.13 us
    all_to_all x1, starting transfers between devices, shards(): lax.all_to_all(partial_value.reshape(owners, CAP, width), 'expert', split...  5.52 us
    all_to_all x1, waiting for transfers between devices, shards(): lax.all_to_all(partial_value.reshape(owners, CAP, width), 'expert', split...  5.08 us
  transfers between devices with their start and end apart: 8, of which 7 were waited for; matrix products, arithmetic and copies ran while one was open for 10% of the time, Pallas kernels for 0%

commit v1 on v0

--- a/solution.py
+++ b/solution.py
@@ -97,7 +97,8 @@
     down_local = lax.dot_general(
         hidden, scaled, (((0,), (0,)), ((), ())), preferred_element_type=jnp.float32
     )
-    down_grad = lax.psum(down_local.astype(jnp.bfloat16), "replica")[None]
+    perform_shapes = lambda x_in: jnp.sum(lax.all_gather(x_in, "replica"), axis=0)
+    down_grad = perform_shapes(down_local.astype(jnp.bfloat16))[None]
     return (x_grad, gate_grad, up_grad, down_grad)
 
 

time: 172 us -> 178 us (1.035)
  blocking collectives: 0 us -> 12.2 us
  other arithmetic: 3.13 us -> 8.8 us
  starting transfers between devices: 16.4 us -> 10.9 us
  local copies, waits for them, and re-layouts: 9.59 us -> 5.02 us
  waiting for transfers between devices: 115 us -> 113 us
    all_gather x0 -> x1, waiting for transfers between devices: none -> 46.3 us  [shards(): lax.all_gather(x_in, 'replica')]
    psum x1 -> x0, waiting for transfers between devices: 43.6 us -> none  [shards(): down_grad = lax.psum(down_local.astype(jnp.bfloat16), 'replica')[None]]
    all_to_all x0 -> x1, blocking collectives: none -> 12.2 us  [shards(): lax.all_to_all(partial_value.reshape(owners, CAP, width), 'expert', split...]
    reduce_sum x0 -> x1, other arithmetic: none -> 5.66 us  [shards(): jnp.sum(lax.all_gather(x_in, 'replica'), axis=0)]
    all_to_all x1 -> x0, starting transfers between devices: 5.52 us -> none  [shards(): lax.all_to_all(partial_value.reshape(owners, CAP, width), 'expert', split...]
    all_to_all x1 -> x0, waiting for transfers between devices: 5.08 us -> none  [shards(): lax.all_to_all(partial_value.reshape(owners, CAP, width), 'expert', split...]
    unnamed x5 -> x4, local copies, waits for them, and re-layouts: 4.58 us -> 0.65 us
  transfers between devices with their start and end apart: 8 -> 7, of which waited for: 7 -> 6; matrix products, arithmetic and copies ran while one was open for 10% -> 9% of each run, Pallas kernels for 0% -> 0%
where the time goes in v1:
time: 178 us; the launch traced here: 177 us
  waiting for transfers between devices  113 us (63%)
  between operations  13.9 us (8%)
  matrix products  13.8 us (8%)
  blocking collectives  12.2 us (7%)
  starting transfers between devices  10.9 us (6%)
  other arithmetic  8.8 us (5%)
  local copies, waits for them, and re-layouts  5.02 us (3%)
    all_gather x1, waiting for transfers between devices, shards(): lax.all_gather(x_in, 'replica')  46.3 us
    reduce_scatter x1, waiting for transfers between devices, shards(): lax.psum_scatter(lax.dot_general(inputs, both_back, (((0,), (0,)), ((), (...  20.7 us
    all_gather x1, waiting for transfers between devices, shards(): lax.all_gather(w_gate, 'replica', axis=1, tiled=True)  19.3 us
    all_gather x1, waiting for transfers between devices, shards(): lax.all_gather(w_down, 'replica', axis=2, tiled=True)  12.4 us
    all_to_all x1, blocking collectives, shards(): lax.all_to_all(partial_value.reshape(owners, CAP, width), 'expert', split...  12.2 us
    all_to_all x1, starting transfers between devices, shards(): lax.all_to_all(send_weight, 'expert', split_axis=0, concat_axis=0, tiled=...  7.31 us
    all_to_all x1, waiting for transfers between devices, shards(): lax.all_to_all(send_rows, 'expert', split_axis=0, concat_axis=0, tiled=True)  7.13 us
    reduce_sum x1, other arithmetic, shards(): jnp.sum(lax.all_gather(x_in, 'replica'), axis=0)  5.66 us
  transfers between devices with their start and end apart: 7, of which 6 were waited for; matrix products, arithmetic and copies ran while one was open for 9% of the time, Pallas kernels for 0%

profile of v1, /device:TPU:0, one launch (start us, length us, event | category | flops | bytes accessed | tf_op | source)
XLA Modules:
  0.0 177.5 jit_solution(16903601143496379427)
XLA Ops:
  7.2 0.7 all-gather.8.cloned.1.call-update
  7.9 0.7 all-gather.6.cloned.1.call-update
  8.7 0.7 all-gather.10.cloned.1.call-update
  9.4 0.7 convert_element_type.63
  10.0 0.7 convert_reduce_fusion.1
  10.8 0.2 reduce_window_sum.11
  11.1 0.8 select_reduce_fusion.2
  11.9 0.7 compare_select_fusion
  12.6 0.1 select_reduce_fusion
  13.0 0.7 copy.30
  13.7 7.3 %all-to-all-start = ((bf16[8,1,2]{2,1,0:T(2,128)(2,1)}), bf16[8,1,2]{2,1,0:T(2,128)(2,1)S(1)}, u32[]{:S(2)}, u32[]{:S(2)}) async-start(bf16[8,1,2]{2,1,0:T(2,128)(2,1)} %copy.30), calls=%async_computation | async-start | bytes 8192 | tf_op jit(solution)/shard_map/all_to_all | solution.py:36
  21.0 1.4 convolution_convert_fusion
  22.6 4.9 %all-to-all-done = bf16[8,1,2]{2,1,0:T(2,128)(2,1)S(1)} async-done(((bf16[8,1,2]{2,1,0:T(2,128)(2,1)}), bf16[8,1,2]{2,1,0:T(2,128)(2,1)S(1)}, u32[]{:S(2)}, u32[]{:S(2)}) %all-to-all-start) | async-done | bytes 64 | tf_op jit(solution)/shard_map/all_to_all | solution.py:36
  27.5 0.7 broadcast_in_dim.47
  28.2 3.4 %all-to-all-start.1 = ((bf16[8,2,4096]{2,1,0:T(2,128)(2,1)}), bf16[8,2,4096]{2,1,0:T(2,128)(2,1)S(1)}, u32[]{:S(2)}, u32[]{:S(2)}) async-start(bf16[8,2,4096]{2,1,0:T(2,128)(2,1)} %bitcast), calls=%async_computation.1 | async-start | bytes 262144 | tf_op jit(solution)/shard_map/all_to_all | solution.py:35
  31.7 7.1 %all-to-all-done.1 = bf16[8,2,4096]{2,1,0:T(2,128)(2,1)S(1)} async-done(((bf16[8,2,4096]{2,1,0:T(2,128)(2,1)}), bf16[8,2,4096]{2,1,0:T(2,128)(2,1)S(1)}, u32[]{:S(2)}, u32[]{:S(2)}) %all-to-all-start.1) | async-done | bytes 131104 | tf_op jit(solution)/shard_map/all_to_all | solution.py:35
  38.9 1.8 %fusion.16 = f32[16,384]{1,0:T(8,128)S(1)} fusion(bf16[16,4096]{1,0:T(8,128)(2,1)S(1)} %reshape.48, bf16[1,2048,384]{2,1,0:T(8,128)(2,1)} %all-gather.8.cloned.1.call-done), kind=kOutput, calls=%fused_computation.21 | convolution fusion | flops 25165824 | bytes 1662976 | tf_op jit(solution)/shard_map/dot_general | solution.py:52
  40.7 12.4 %all-gather.6.cloned.1.call-done = bf16[1,384,2048]{2,1,0:T(8,128)(2,1)} async-done(((bf16[1,384,512]{2,1,0:T(8,128)(2,1)}), bf16[1,384,2048]{2,1,0:T(8,128)(2,1)}) %all-gather.6.cloned.1.call-update) | async-done | bytes 1572880 | tf_op jit(solution)/shard_map/all_gather | solution.py:41
  53.1 1.9 %fusion.8 = f32[16,384]{1,0:T(8,128)S(1)} fusion(bf16[1,384,2048]{2,1,0:T(8,128)(2,1)} %all-gather.6.cloned.1.call-done, bf16[16,4096]{1,0:T(8,128)(2,1)S(1)} %reshape.48, f32[16]{0:T(128)S(1)} %reshape.51), kind=kOutput, calls=%fused_computation.10 | convolution fusion | flops 25264128 | bytes 1663488 | tf_op jit(solution)/shard_map/dot_general | solution.py:57
  55.1 19.3 %all-gather.10.cloned.1.call-done = bf16[1,2048,384]{2,1,0:T(8,128)(2,1)} async-done(((bf16[1,512,384]{2,1,0:T(8,128)(2,1)}), bf16[1,2048,384]{2,1,0:T(8,128)(2,1)}) %all-gather.10.cloned.1.call-update) | async-done | bytes 1572880 | tf_op jit(solution)/shard_map/all_gather | solution.py:39
  74.4 1.7 multiply_convert_fusion.3
  76.1 2.7 %convolution_convert_fusion.1 = bf16[2048,768]{1,0:T(8,128)(2,1)} fusion(bf16[16,4096]{1,0:T(8,128)(2,1)S(1)} %reshape.48, bf16[16,384]{1,0:T(8,128)(2,1)S(1)} %get-tuple-element.11, bf16[16,384]{1,0:T(8,128)(2,1)S(1)} %get-tuple-element.10), kind=kOutput, calls=%fused_computation.1 | convolution fusion | flops 51953664 | bytes 3235840 | tf_op jit(solution)/shard_map/dot_general | solution.py:85
  79.0 1.8 convolution_convert_fusion.2
  80.7 0.6 copy-done.1
  81.4 0.9 fusion.5
  82.4 12.2 %all_to_all.19 = bf16[8,2,2048]{2,1,0:T(2,128)(2,1)S(1)} all-to-all(bf16[8,2,2048]{2,1,0:T(2,128)(2,1)S(1)} %reshape.49), channel_id=1, replica_groups=mesh['expert'=8,'replica'=4] {'expert'}, dimensions={0} | all-to-all | bytes 131072 | tf_op jit(solution)/shard_map/all_to_all | solution.py:67
  94.7 0.3 fusion.28
  95.0 1.1 fusion.4
  96.2 20.7 %reduce-scatter.2.cloned.1.call-done = bf16[512,768]{1,0:T(8,128)(2,1)} async-done(((bf16[2048,768]{1,0:T(8,128)(2,1)}), bf16[512,768]{1,0:T(8,128)(2,1)}) %reduce-scatter.2.cloned.1.call-update) | async-done | bytes 786448 | tf_op jit(solution)/shard_map/reduce_scatter | solution.py:84
  116.9 2.1 %slice_bitcast_fusion = (bf16[1,512,384]{2,1,0:T(8,128)(2,1)}, bf16[1,512,384]{2,1,0:T(8,128)(2,1)}) fusion(bf16[512,768]{1,0:T(8,128)(2,1)} %reduce-scatter.2.cloned.1.call-done), kind=kLoop, calls=%fused_computation.15 | loop fusion | bytes 1572864 | tf_op jit(solution)/shard_map/broadcast_in_dim | solution.py:96
  119.0 46.3 %all-gather.12.cloned.1.call-done = bf16[1536,2048]{1,0:T(8,128)(2,1)} async-done(((bf16[384,2048]{1,0:T(8,128)(2,1)}), bf16[1536,2048]{1,0:T(8,128)(2,1)}) %all-gather.12.cloned.1.call-update) | async-done | bytes 6291472 | tf_op jit(solution)/shard_map/all_gather | solution.py:100
  165.3 5.7 %reduce_sum.52 = bf16[384,2048]{1,0:T(8,128)(2,1)} reduce(bf16[4,384,2048]{2,1,0:T(8,128)(2,1)} %bitcast.26, bf16[]{:T(256)} %constant.20.clone.1), dimensions={0}, to_apply=%region_7.8 | reduce | flops 2359296 | bytes 7864322 | tf_op jit(solution)/shard_map/reduce_sum | solution.py:100
  (26 shorter events, 1.2 us)
Async XLA Ops:
  7.2 31.8 %all-gather.8.cloned.1.call-start = ((), (), s32[]{:S(2)}) async-start(), calls=%async_computation.5 | async-start | bytes 1966080 | tf_op jit(solution)/shard_map/all_gather | solution.py:40
  7.9 45.2 %all-gather.6.cloned.1.call-start = ((), (), s32[]{:S(2)}) async-start(), calls=%async_computation.4 | async-start | bytes 1966080 | tf_op jit(solution)/shard_map/all_gather | solution.py:41
  8.6 65.7 %all-gather.10.cloned.1.call-start = ((), (), s32[]{:S(2)}) async-start(), calls=%async_computation.6 | async-start | bytes 1966080 | tf_op jit(solution)/shard_map/all_gather | solution.py:39
  13.7 13.7 %all-to-all-start = ((bf16[8,1,2]{2,1,0:T(2,128)(2,1)}), bf16[8,1,2]{2,1,0:T(2,128)(2,1)S(1)}, u32[]{:S(2)}, u32[]{:S(2)}) async-start(bf16[8,1,2]{2,1,0:T(2,128)(2,1)} %copy.30), calls=%async_computation | async-start | bytes 8192 | tf_op jit(solution)/shard_map/all_to_all | solution.py:36
  28.2 10.7 %all-to-all-start.1 = ((bf16[8,2,4096]{2,1,0:T(2,128)(2,1)}), bf16[8,2,4096]{2,1,0:T(2,128)(2,1)S(1)}, u32[]{:S(2)}, u32[]{:S(2)}) async-start(bf16[8,2,4096]{2,1,0:T(2,128)(2,1)} %bitcast), calls=%async_computation.1 | async-start | bytes 262144 | tf_op jit(solution)/shard_map/all_to_all | solution.py:35
  31.6 85.4 %reduce-scatter.2.cloned.1.call-start = ((), (), s32[]{:S(2)}) async-start(), calls=%async_computation.7 | async-start | bytes 3932160 | tf_op jit(solution)/shard_map/reduce_scatter | solution.py:84
  78.9 86.4 %all-gather.12.cloned.1.call-start = ((), (), s32[]{:S(2)}) async-start(), calls=%async_computation.8 | async-start | bytes 7864320 | tf_op jit(solution)/shard_map/all_gather | solution.py:100
  78.9 1.8 %copy-start = (bf16[1,2048,384]{2,1,0:T(8,128)(2,1)S(1)}, bf16[1,2048,384]{2,1,0:T(8,128)(2,1)}, u32[]{:S(2)}) copy-start(bf16[1,2048,384]{2,1,0:T(8,128)(2,1)} %all-gather.8.cloned.1.call-done) | copy-start | bytes 4718596
  78.9 2.4 %copy-start.1 = (bf16[1,2048,384]{2,1,0:T(8,128)(2,1)S(1)}, bf16[1,2048,384]{2,1,0:T(8,128)(2,1)}, u32[]{:S(2)}) copy-start(bf16[1,2048,384]{2,1,0:T(8,128)(2,1)} %all-gather.10.cloned.1.call-done) | copy-start | bytes 4718596
Sparse Core Ops, SparseCore 0:
  9.5 22.3 all-gather.7
  33.5 19.6 all-gather.5
  54.7 19.6 all-gather.9
  79.0 37.8 reduce-scatter.1
  118.9 46.3 all-gather.11
